TPU v7x, 512 devices: a whole 4x4x16 slice. The times are simulated.
512 devices in a mesh: group: 16 (over x, z_hi), shard: 32 (over z_lo, y, core).
Axes of the slice: x: 4, y: 4, z: 16 (z_hi: 4, z_lo: 4; z = z_hi * 4 + z_lo), core: 2. Of those that a mesh axis runs over, the one named last changes fastest.
Arguments:
- step_count: int32 [1], replicated, may hold values from 2 to 8
- block_order: int32 [224], replicated, may hold values from 0 to 223, as said below
- saved_tiles: bfloat16 [512, 4, 18, 18, 256], P(('group', 'shard')), may hold values from -6 to 6
- pre_act: bfloat16 [262144, 256], P(('group', 'shard')), may hold values from -6 to 6
- grad_output: bfloat16 [262144, 256], P(('group', 'shard')), may hold values from -0.0234375 to 0.0234375
- pointwise_live: bfloat16 [256, 256], replicated, may hold values from -0.375 to 0.375
- master_rows: float32 [7168, 256], P('shard'), may hold values from -0.25 to 0.25, as said below
- row_moment: float32 [7168], P('shard'), may hold values from 0.5 to 30, as said below
- col_moment: float32 [2, 256], replicated, may hold values from 0.03 to 0.3
- next_tiles: bfloat16 [512, 4, 18, 18, 256], P(('group', 'shard')), may hold values from -6 to 6
Outputs:
- update_rows: float32 [7168, 256], P('shard')
- new_master: float32 [7168, 256], P('shard')
- new_row_moment: float32 [7168], P('shard')
- new_col_moment: float32 [2, 256], replicated
- next_output: bfloat16 [262144, 256], P(('group', 'shard'))
Inputs may be any that keep to these rules, and one draw needn't show every extreme that they name: `block_order`: a permutation of 0 to 223. `master_rows`: rows of the 3x3x3 kernel are of order (6912) ** -0.5 and rows of the 1x1x1 kernel of order 256 ** -0.5. `row_moment`: positive row factors.
All inputs are finite; a program needn't handle non-finite values.
Results may differ from a plain program's by a relative error of at most 0.023.
Values may be sent and summed in bfloat16 or wider, within the bound.
A program may use at most 64 MiB of HBM per device.

v0:
```python
import jax
import jax.numpy as jnp
from jax import lax
from jax.sharding import PartitionSpec as P

CI = 256
CO = 256
BLK = 32
FR = 2
HW = 16
NB3 = 216
NB = 224
learn_rate = 0.002
decay_power = 0.8


def silu_slope(values):
    sigma = jax.nn.sigmoid(values)
    return sigma * (1.0 + values * (1.0 - sigma))


def tap_views(frames):
    views = []
    for frame_off in range(3):
        for row_off in range(3):
            for col_off in range(3):
                window = frames[
                    frame_off : frame_off + FR, row_off : row_off + HW, col_off : col_off + HW, :
                ]
                views.append(window.reshape(FR * HW * HW, CI))
    return views


def contract_rows(left, right):
    return lax.dot_general(
        left, right, (((0,), (0,)), ((), ())), preferred_element_type=jnp.float32
    )


def kernel_sums(values, is_small):
    large_part = jnp.sum(jnp.where(is_small[:, None], 0.0, values), axis=0)
    small_part = jnp.sum(jnp.where(is_small[:, None], values, 0.0), axis=0)
    return jnp.stack([large_part, small_part])


def shards(
    step_count,
    block_order,
    saved_tiles,
    pre_act,
    grad_output,
    pointwise_live,
    master_rows,
    row_moment,
    col_moment,
    next_tiles,
):
    pre_float = pre_act.astype(jnp.float32)
    activation = jax.nn.silu(pre_float).astype(jnp.bfloat16)
    grad_act = lax.dot_general(
        grad_output, pointwise_live, (((1,), (1,)), ((), ())), preferred_element_type=jnp.float32
    )
    grad_pre = (grad_act * silu_slope(pre_float)).astype(jnp.bfloat16)
    pieces = [contract_rows(view, grad_pre) for view in tap_views(saved_tiles[0])]
    pieces.append(contract_rows(activation, grad_output))
    own_term = jnp.concatenate(pieces, axis=0).astype(jnp.bfloat16)
    total_rows = NB * BLK
    stored = jnp.take(own_term.reshape(NB, BLK, CO), block_order, axis=0).reshape(total_rows, CO)
    own_rows = master_rows.shape[0]
    partial_value = lax.psum_scatter(stored, "shard", scatter_dimension=0, tiled=True).astype(
        jnp.float32
    )
    gradient = lax.psum(partial_value, "group")
    owner = lax.axis_index("shard")
    own_count = own_rows // BLK
    own_blocks = lax.dynamic_slice_in_dim(block_order, owner * own_count, own_count)
    is_small = jnp.repeat(own_blocks >= NB3, BLK, total_repeat_length=own_rows)
    decay_rate = 1.0 - step_count.astype(jnp.float32)[0] ** (-decay_power)
    counts = jnp.array([27 * CI, CO], jnp.float32)
    squares = gradient * gradient
    new_row = decay_rate * row_moment + (1.0 - decay_rate) * jnp.mean(squares, axis=1)
    col_part = kernel_sums(squares, is_small)
    row_part = kernel_sums(new_row[:, None], is_small)[:, 0]
    col_total, row_total = lax.psum((col_part, row_part), "shard")
    new_col = decay_rate * col_moment + (1.0 - decay_rate) * col_total / counts[:, None]
    row_mean = row_total / counts
    col_rows = jnp.where(is_small[:, None], new_col[1], new_col[0])
    mean_rows = jnp.where(is_small, row_mean[1], row_mean[0])
    scaled = gradient / jnp.sqrt(new_row[:, None] * col_rows / mean_rows[:, None])
    square_part = kernel_sums(jnp.sum(scaled * scaled, axis=1)[:, None], is_small)[:, 0]
    square_total = lax.psum(square_part, "shard")
    clip_factor = jnp.maximum(1.0, jnp.sqrt(square_total / (counts * CO)))
    update_rows = scaled / jnp.where(is_small, clip_factor[1], clip_factor[0])[:, None]
    new_master = master_rows - learn_rate * update_rows
    weights_low = new_master.astype(jnp.bfloat16)
    gathered = lax.all_gather(weights_low, "shard", axis=0, tiled=True)
    inverse = jnp.zeros((NB,), jnp.int32).at[block_order].set(jnp.arange(NB, dtype=jnp.int32))
    natural = jnp.take(gathered.reshape(NB, BLK, CO), inverse, axis=0).reshape(total_rows, CO)
    spatial = natural[: 27 * CI].reshape(27, CI, CO)
    pointwise = natural[27 * CI :]
    hidden_sum = jnp.zeros((FR * HW * HW, CO), jnp.float32)
    for index_tap, view in enumerate(tap_views(next_tiles[0])):
        hidden_sum = hidden_sum + jnp.dot(
            view, spatial[index_tap], preferred_element_type=jnp.float32
        )
    hidden_act = jax.nn.silu(hidden_sum).astype(jnp.bfloat16)
    next_output = jnp.dot(hidden_act, pointwise, preferred_element_type=jnp.float32).astype(
        jnp.bfloat16
    )
    return (update_rows, new_master, new_row, new_col, next_output)


def solution(mesh):
    in_specs = (
        P(),
        P(),
        P(("group", "shard"), None, None, None, None),
        P(("group", "shard"), None),
        P(("group", "shard"), None),
        P(),
        P("shard", None),
        P("shard"),
        P(),
        P(("group", "shard"), None, None, None, None),
    )
    out_specs = (P("shard", None), P("shard", None), P("shard"), P(), P(("group", "shard"), None))
    return jax.shard_map(shards, mesh=mesh, in_specs=in_specs, out_specs=out_specs, check_vma=False)
```

profile of v0, /device:TPU:1, one launch (start us, length us, event | category | flops | bytes accessed | tf_op | source)
XLA Modules:
  0.0 556.7 jit_solution(18183779678937260853)
XLA Ops:
  7.2 1.3 copy.102
  16.6 0.9 fusion.28
  23.1 0.9 fusion.42
  25.9 0.9 fusion.48
  27.8 0.9 fusion.52
  32.5 0.9 fusion.62
  35.3 1.0 fusion.12
  36.3 4.9 gather_fusion
  41.2 3.8 broadcast_select_fusion.1
  46.8 4.5 select_select_fusion
  51.3 150.8 %reduce-scatter.2.cloned.1.call-done = bf16[224,256]{1,0:T(8,128)(2,1)} async-done(((bf16[7168,256]{1,0:T(8,128)(2,1)}), bf16[224,256]{1,0:T(8,128)(2,1)}) %reduce-scatter.2.cloned.1.call-update) | async-done | bytes 114704 | tf_op jit(solution)/shard_map/reduce_scatter | solution.py:70
  202.1 89.2 %all-reduce.2 = f32[224,256]{1,0:T(8,128)S(1)} all-reduce(bf16[224,256]{1,0:T(8,128)(2,1)} %reduce-scatter.2.cloned.1.call-done), channel_id=1, replica_groups=mesh['group'=16,'shard'=32] {'group'}, use_global_device_ids=true, to_apply=%region_1.3 | all-reduce | flops 57344 | bytes 344064 | tf_op jit(solution)/shard_map/psum | solution.py:73
  291.5 5.2 select_reduce_fusion.5
  296.7 1.3 maximum_bitcast_fusion
  298.0 84.7 %all-reduce = (f32[2]{0:T(128)S(1)}, f32[2,256]{1,0:T(2,128)S(1)}) all-reduce(f32[2]{0:T(128)S(1)} %maximum_bitcast_fusion, f32[2,256]{1,0:T(2,128)S(1)} %pad_maximum_fusion), channel_id=1, replica_groups=mesh['group'=16,'shard'=32] {'shard'}, use_global_device_ids=true, to_apply=%region_8.10 | all-reduce | flops 514 | bytes 4112 | tf_op jit(solution)/shard_map/psum | solution.py:84
  383.3 5.7 %broadcast_select_fusion.3 = f32[224]{0:T(256)S(1)} fusion(f32[]{:T(128)} %bitcast.74, f32[]{:T(128)} %bitcast.73, pred[]{:T(512)} %bitcast.65, pred[]{:T(512)} %bitcast.64, pred[]{:T(512)} %bitcast.63, pred[]{:T(512)} %bitcast.62, pred[]{:T(512)} %bitcast.61, pred[]{:T(512)} %bitcast.60, pred[]{:T(512)} %bitcast.59, s32[256]{0:T(256)S(1)} %add_bitcast_fusion), kind=kLoop, calls=%fused_computation.172 | loop fusion | flops 4704 | bytes 1807 | tf_op jit(solution)/shard_map/jit(_where)/select_n | solution.py:88
  389.3 5.2 select_reduce_fusion.3
  394.5 1.3 maximum_bitcast_fusion.1
  395.8 67.4 %psum.31 = f32[2]{0:T(128)S(1)} all-reduce(f32[2]{0:T(128)S(1)} %maximum_bitcast_fusion.1), channel_id=1, replica_groups=mesh['group'=16,'shard'=32] {'shard'}, use_global_device_ids=true, to_apply=%region_12.14 | all-reduce | flops 2 | bytes 16 | tf_op jit(solution)/shard_map/psum | solution.py:91
  463.8 5.7 %broadcast_select_fusion.2 = f32[224]{0:T(256)S(1)} fusion(f32[]{:T(128)} %bitcast.79, f32[]{:T(128)} %bitcast.78, pred[]{:T(512)} %bitcast.65, pred[]{:T(512)} %bitcast.64, pred[]{:T(512)} %bitcast.63, pred[]{:T(512)} %bitcast.62, pred[]{:T(512)} %bitcast.61, pred[]{:T(512)} %bitcast.60, pred[]{:T(512)} %bitcast.59, s32[256]{0:T(256)S(1)} %add_bitcast_fusion), kind=kLoop, calls=%fused_computation.171 | loop fusion | flops 4704 | bytes 1807 | tf_op jit(solution)/shard_map/jit(_where)/select_n | solution.py:93
  470.5 1.5 scatter_custom_fusion
  472.1 1.4 fusion.85
  473.5 2.1 fusion.84
  475.6 53.3 %all-gather.2.cloned.1.call-done = bf16[7168,256]{1,0:T(8,128)(2,1)} async-done(((bf16[224,256]{1,0:T(8,128)(2,1)}), bf16[7168,256]{1,0:T(8,128)(2,1)}) %all-gather.2.cloned.1.call-update) | async-done | bytes 3670032 | tf_op jit(solution)/shard_map/all_gather | solution.py:96
  528.9 4.9 gather_fusion.1
  533.8 2.5 broadcast_select_fusion
  536.4 1.0 fusion.82
  539.0 1.0 convolution_bitcast_fusion.6
  540.1 1.0 convolution_bitcast_fusion.7
  541.1 1.1 convolution_bitcast_fusion.8
  545.9 1.1 fusion.10
  547.0 2.9 convolution_convert_fusion
  (140 shorter events, 30.9 us)
Async XLA Ops:
  7.2 2.3 copy-start
  7.2 194.9 %reduce-scatter.2.cloned.1.call-start = ((), (), s32[]{:S(2)}) async-start(), calls=%async_computation.1 | async-start | bytes 3784704 | tf_op jit(solution)/shard_map/reduce_scatter | solution.py:70
  45.0 1.8 copy-start.28
  45.0 246.5 %copy-start.26 = (f32[224]{0:T(256)S(1)}, f32[224]{0:T(256)}, u32[]{:S(2)}) copy-start(f32[224]{0:T(256)} %param.22) | copy-start | bytes 2692
  45.0 337.7 %copy-start.25 = (f32[2,256]{1,0:T(2,128)S(1)}, f32[2,256]{1,0:T(2,128)}, u32[]{:S(2)}) copy-start(f32[2,256]{1,0:T(2,128)} %param.23) | copy-start | bytes 6148
  45.0 337.7 %copy-start.29 = (f32[2]{0:T(128)S(1)}, f32[2]{0:T(128)}, u32[]{:S(2)}) copy-start(f32[2]{0:T(128)} %constant.126) | copy-start | bytes 28
  45.0 418.2 %copy-start.32 = (f32[2]{0:T(128)S(1)}, f32[2]{0:T(128)}, u32[]{:S(2)}) copy-start(f32[2]{0:T(128)} %constant.129) | copy-start | bytes 28
  45.0 424.5 %copy-start.22 = (f32[224,256]{1,0:T(8,128)S(1)}, f32[224,256]{1,0:T(8,128)}, u32[]{:S(2)}) copy-start(f32[224,256]{1,0:T(8,128)} %param.21) | copy-start | bytes 688132
  45.0 426.9 %copy-start.21 = (bf16[1,4,18,18,256]{4,1,3,2,0:T(4,128)(2,1)S(1)}, bf16[1,4,18,18,256]{4,1,3,2,0:T(4,128)(2,1)}, u32[]{:S(2)}) copy-start(bf16[1,4,18,18,256]{4,1,3,2,0:T(4,128)(2,1)} %param.24) | copy-start | bytes 1990660
  45.0 483.9 %all-gather.2.cloned.1.call-start = ((), (), s32[]{:S(2)}) async-start(), calls=%async_computation.2 | async-start | bytes 3784704 | tf_op jit(solution)/shard_map/all_gather | solution.py:96
  296.7 176.9 %copy-start.24 = (f32[224]{0:T(256)}, f32[224]{0:T(256)S(1)}, u32[]{:S(2)}) copy-start(f32[224]{0:T(256)S(1)} %get-tuple-element.32) | copy-start | bytes 2692
  382.7 90.8 %copy-start.23 = (f32[2,256]{1,0:T(2,128)}, f32[2,256]{1,0:T(2,128)S(1)}, u32[]{:S(2)}) copy-start(f32[2,256]{1,0:T(2,128)S(1)} %multiply_add_fusion) | copy-start | bytes 6148
  537.4 1.4 copy-start.4
  537.4 1.7 copy-start.3
  537.4 2.7 copy-start.2
  537.6 3.5 copy-start.1
  537.8 4.3 copy-start.20
  538.3 4.1 copy-start.19
  538.5 4.1 copy-start.18
  539.0 3.9 copy-start.17
  540.1 3.1 copy-start.16
  542.2 1.3 copy-start.14
  542.4 1.3 copy-start.12
  542.6 1.3 copy-start.15
  542.9 1.3 copy-start.13
  543.2 1.3 copy-start.11
  543.4 1.3 copy-start.10
  543.7 1.3 copy-start.9
  543.9 1.3 copy-start.8
  544.2 1.2 copy-start.7
  544.4 1.2 copy-start.6
  544.7 1.2 copy-start.5
  (3 other events, 2.6 us)
Sparse Core Ops, SparseCore 0:
  45.2 156.8 reduce-scatter.1
  470.6 58.3 all-gather.1
where the time goes:
time: 557 us
  blocking collectives  241 us (43%)
  waiting for transfers between devices  204 us (37%)
  matrix products  38.5 us (7%)
  other arithmetic  36.8 us (7%)
  local copies, waits for them, and re-layouts  20.3 us (4%)
  between operations  15.6 us (3%)
    reduce_scatter x1, waiting for transfers between devices, shards(): lax.psum_scatter(stored, 'shard', scatter_dimension=0, tiled=True)  151 us
    psum x1, blocking collectives, shards(): gradient = lax.psum(partial_value, 'group')  89.2 us
    psum x1, blocking collectives, shards(): col_total, row_total = lax.psum((col_part, row_part), 'shard')  84.7 us
    psum x1, blocking collectives, shards(): square_total = lax.psum(square_part, 'shard')  67.4 us
    all_gather x1, waiting for transfers between devices, shards(): gathered = lax.all_gather(weights_low, 'shard', axis=0, tiled=True)  53.3 us
    dot_general x28, matrix products, contract_rows(): lax.dot_general(left, right, (((0,), (0,)), ((), ())), preferred_element_...  26.2 us
  transfers between devices with their start and end apart: 2, of which 2 were waited for; matrix products, arithmetic and copies ran while one was open for 2% of the time, Pallas kernels for 0%

commit v1 on v0

--- a/solution.py
+++ b/solution.py
@@ -93,7 +93,9 @@
     update_rows = scaled / jnp.where(is_small, clip_factor[1], clip_factor[0])[:, None]
     new_master = master_rows - learn_rate * update_rows
     weights_low = new_master.astype(jnp.bfloat16)
-    gathered = lax.all_gather(weights_low, "shard", axis=0, tiled=True)
+    gathered = jnp.concatenate(
+        lax.all_to_all(jnp.stack([weights_low] * lax.axis_size("shard")), "shard", 0, 0), axis=0
+    )
     inverse = jnp.zeros((NB,), jnp.int32).at[block_order].set(jnp.arange(NB, dtype=jnp.int32))
     natural = jnp.take(gathered.reshape(NB, BLK, CO), inverse, axis=0).reshape(total_rows, CO)
     spatial = natural[: 27 * CI].reshape(27, CI, CO)

time: 557 us -> 586 us (1.052)
  waiting for transfers between devices: 204 us -> 228 us
    all_to_all x0 -> x1, waiting for transfers between devices: none -> 76.8 us  [shards(): lax.all_to_all(jnp.stack([weights_low] * lax.axis_size('shard')), 'shard'...]
    all_gather x1 -> x0, waiting for transfers between devices: 53.3 us -> none  [shards(): gathered = lax.all_gather(weights_low, 'shard', axis=0, tiled=True)]
where the time goes in v1:
time: 586 us
  blocking collectives  240 us (41%)
  waiting for transfers between devices  228 us (39%)
  matrix products  38.7 us (7%)
  other arithmetic  36.2 us (6%)
  local copies, waits for them, and re-layouts  22.6 us (4%)
  between operations  15.5 us (3%)
    reduce_scatter x1, waiting for transfers between devices, shards(): lax.psum_scatter(stored, 'shard', scatter_dimension=0, tiled=True)  151 us
    psum x1, blocking collectives, shards(): gradient = lax.psum(partial_value, 'group')  88.5 us
    psum x1, blocking collectives, shards(): col_total, row_total = lax.psum((col_part, row_part), 'shard')  83.9 us
    all_to_all x1, waiting for transfers between devices, shards(): lax.all_to_all(jnp.stack([weights_low] * lax.axis_size('shard')), 'shard'...  76.8 us
    psum x1, blocking collectives, shards(): square_total = lax.psum(square_part, 'shard')  67.4 us
    dot_general x28, matrix products, contract_rows(): lax.dot_general(left, right, (((0,), (0,)), ((), ())), preferred_element_...  26.4 us
  transfers between devices with their start and end apart: 2, of which 2 were waited for; matrix products, arithmetic and copies ran while one was open for 2% of the time, Pallas kernels for 0%

profile of v1, /device:TPU:1, one launch (start us, length us, event | category | flops | bytes accessed | tf_op | source)
XLA Modules:
  0.0 585.7 jit_solution(4013844934246655540)
XLA Ops:
  7.2 1.3 copy.102
  23.2 1.0 fusion.42
  29.8 1.0 fusion.56
  32.6 1.0 fusion.62
  35.4 1.0 fusion.12
  36.4 4.9 gather_fusion
  41.3 3.8 broadcast_select_fusion.1
  46.8 4.5 select_select_fusion
  51.2 151.0 %reduce-scatter.2.cloned.1.call-done = bf16[224,256]{1,0:T(8,128)(2,1)} async-done(((bf16[7168,256]{1,0:T(8,128)(2,1)}), bf16[224,256]{1,0:T(8,128)(2,1)}) %reduce-scatter.2.cloned.1.call-update) | async-done | bytes 114704 | tf_op jit(solution)/shard_map/reduce_scatter | solution.py:70
  202.2 88.5 %all-reduce.2 = f32[224,256]{1,0:T(8,128)S(1)} all-reduce(bf16[224,256]{1,0:T(8,128)(2,1)} %reduce-scatter.2.cloned.1.call-done), channel_id=1, replica_groups=mesh['group'=16,'shard'=32] {'group'}, use_global_device_ids=true, to_apply=%region_1.3 | all-reduce | flops 57344 | bytes 344064 | tf_op jit(solution)/shard_map/psum | solution.py:73
  290.9 5.1 select_reduce_fusion.5
  296.0 1.3 maximum_bitcast_fusion
  297.2 83.9 %all-reduce = (f32[2]{0:T(128)S(1)}, f32[2,256]{1,0:T(2,128)S(1)}) all-reduce(f32[2]{0:T(128)S(1)} %maximum_bitcast_fusion, f32[2,256]{1,0:T(2,128)S(1)} %pad_maximum_fusion), channel_id=1, replica_groups=mesh['group'=16,'shard'=32] {'shard'}, use_global_device_ids=true, to_apply=%region_8.10 | all-reduce | flops 514 | bytes 4112 | tf_op jit(solution)/shard_map/psum | solution.py:84
  381.8 5.6 broadcast_select_fusion.3
  387.7 5.1 select_reduce_fusion.3
  392.8 1.3 maximum_bitcast_fusion.1
  394.0 67.4 %psum.31 = f32[2]{0:T(128)S(1)} all-reduce(f32[2]{0:T(128)S(1)} %maximum_bitcast_fusion.1), channel_id=1, replica_groups=mesh['group'=16,'shard'=32] {'shard'}, use_global_device_ids=true, to_apply=%region_12.14 | all-reduce | flops 2 | bytes 16 | tf_op jit(solution)/shard_map/psum | solution.py:91
  462.0 5.6 broadcast_select_fusion.2
  468.5 2.3 stack.29
  470.8 5.2 all-to-all-start
  476.0 1.5 scatter_custom_fusion
  477.7 1.4 fusion.85
  479.1 2.1 fusion.84
  481.2 76.8 %all-to-all-done = bf16[32,224,256]{2,1,0:T(8,128)(2,1)} async-done(((bf16[32,224,256]{2,1,0:T(8,128)(2,1)}), bf16[32,224,256]{2,1,0:T(8,128)(2,1)}, u32[]{:S(2)}, u32[]{:S(2)}) %all-to-all-start) | async-done | bytes 3670048 | tf_op jit(solution)/shard_map/all_to_all | solution.py:97
  557.9 4.9 gather_fusion.1
  562.8 2.5 broadcast_select_fusion
  565.4 1.0 fusion.82
  568.0 1.0 convolution_bitcast_fusion.6
  569.1 1.0 convolution_bitcast_fusion.7
  570.1 1.1 convolution_bitcast_fusion.8
  574.9 1.1 fusion.10
  576.0 2.9 convolution_convert_fusion
  (140 shorter events, 32.8 us)
Async XLA Ops:
  7.2 2.3 copy-start
  7.2 195.0 %reduce-scatter.2.cloned.1.call-start = ((), (), s32[]{:S(2)}) async-start(), calls=%async_computation.2 | async-start | bytes 3784704 | tf_op jit(solution)/shard_map/reduce_scatter | solution.py:70
  45.1 1.6 copy-start.28
  45.1 245.8 %copy-start.26 = (f32[224]{0:T(256)S(1)}, f32[224]{0:T(256)}, u32[]{:S(2)}) copy-start(f32[224]{0:T(256)} %param.22) | copy-start | bytes 2692
  45.1 336.0 %copy-start.25 = (f32[2,256]{1,0:T(2,128)S(1)}, f32[2,256]{1,0:T(2,128)}, u32[]{:S(2)}) copy-start(f32[2,256]{1,0:T(2,128)} %param.23) | copy-start | bytes 6148
  45.1 336.0 %copy-start.29 = (f32[2]{0:T(128)S(1)}, f32[2]{0:T(128)}, u32[]{:S(2)}) copy-start(f32[2]{0:T(128)} %constant.126) | copy-start | bytes 28
  45.1 416.3 %copy-start.32 = (f32[2]{0:T(128)S(1)}, f32[2]{0:T(128)}, u32[]{:S(2)}) copy-start(f32[2]{0:T(128)} %constant.129) | copy-start | bytes 28
  45.1 422.6 %copy-start.22 = (f32[224,256]{1,0:T(8,128)S(1)}, f32[224,256]{1,0:T(8,128)}, u32[]{:S(2)}) copy-start(f32[224,256]{1,0:T(8,128)} %param.21) | copy-start | bytes 688132
  296.0 174.8 %copy-start.24 = (f32[224]{0:T(256)}, f32[224]{0:T(256)S(1)}, u32[]{:S(2)}) copy-start(f32[224]{0:T(256)S(1)} %get-tuple-element.32) | copy-start | bytes 2692
  381.2 89.6 %copy-start.23 = (f32[2,256]{1,0:T(2,128)}, f32[2,256]{1,0:T(2,128)S(1)}, u32[]{:S(2)}) copy-start(f32[2,256]{1,0:T(2,128)S(1)} %multiply_add_fusion) | copy-start | bytes 6148
  470.8 6.7 %copy-start.21 = (bf16[1,4,18,18,256]{4,1,3,2,0:T(4,128)(2,1)S(1)}, bf16[1,4,18,18,256]{4,1,3,2,0:T(4,128)(2,1)}, u32[]{:S(2)}) copy-start(bf16[1,4,18,18,256]{4,1,3,2,0:T(4,128)(2,1)} %param.24) | copy-start | bytes 1990660
  470.8 87.1 %all-to-all-start = ((bf16[32,224,256]{2,1,0:T(8,128)(2,1)}), bf16[32,224,256]{2,1,0:T(8,128)(2,1)}, u32[]{:S(2)}, u32[]{:S(2)}) async-start(bf16[32,224,256]{2,1,0:T(8,128)(2,1)} %stack.29), calls=%async_computation.1 | async-start | bytes 7340032 | tf_op jit(solution)/shard_map/all_to_all | solution.py:97
  566.4 1.4 copy-start.4
  566.4 1.7 copy-start.3
  566.4 2.7 copy-start.2
  566.6 3.5 copy-start.1
  566.8 4.3 copy-start.20
  567.3 4.1 copy-start.19
  567.5 4.1 copy-start.18
  568.0 3.9 copy-start.17
  569.1 3.1 copy-start.16
  571.2 1.3 copy-start.14
  571.4 1.3 copy-start.12
  571.6 1.3 copy-start.15
  571.9 1.3 copy-start.13
  572.1 1.3 copy-start.11
  572.4 1.3 copy-start.10
  572.7 1.3 copy-start.9
  572.9 1.3 copy-start.8
  573.2 1.2 copy-start.7
  573.4 1.2 copy-start.6
  573.7 1.2 copy-start.5
  (3 other events, 2.6 us)
Sparse Core Ops, SparseCore 0:
  45.2 156.8 reduce-scatter.1
